TPU v7x, 512 devices: a whole 4x4x16 slice. The times are simulated.
512 devices in a mesh: seq: 32 (over z, core), dp: 16 (over x, y).
Axes of the slice: x: 4, y: 4, z: 16, core: 2. Of those that a mesh axis runs over, the one named last changes fastest.
Arguments:
- queries: bfloat16 [16, 5120, 2048], P('dp', 'seq'), may hold values from -6 to 6
- keys: bfloat16 [16, 5120, 2048], P('dp', 'seq'), may hold values from -6 to 6
- values: bfloat16 [16, 5120, 2048], P('dp', 'seq'), may hold values from -6 to 6
- keep: int32 [16, 5120, 2048], P('dp', 'seq'), may hold values 0 or 1
- gain: float32 [2048], replicated, may hold values from 0.25 to 1.75
- out_weight: bfloat16 [2048, 2048], P(None, 'dp'), may hold values from -0.125 to 0.125
Outputs:
- projected: bfloat16 [16, 5120, 2048], P('dp', 'seq')
All inputs are finite; a program needn't handle non-finite values. No bound on the sum of `keep` on one device may be relied on, other than what follows from the above.
Results may differ from a plain program's by a relative error of at most 0.0051.
Values may be sent and summed in bfloat16 or wider, within the bound.
No kernel may reach another device: no remote copies, remote signals or barrier semaphores. Data moves between devices by JAX's collectives and lax.ppermute only.
A program may use at most 128 MiB of HBM per device.

v0:
```python
import jax
import jax.numpy as jnp
from jax import lax
from jax.sharding import PartitionSpec as P

HEADS = 16
HEAD = 128


def prefix_2(x, axis, combine, identity):
    size, place = (lax.axis_size(axis), lax.axis_index(axis))
    everything = lax.all_gather(x, axis)
    start = jnp.broadcast_to(jnp.asarray(identity, x.dtype), x.shape)

    def turn(k, before):
        reached = k < place
        new = combine(before, everything[k])
        return jnp.where(reached, new, before)

    return lax.fori_loop(0, size, turn, start)


def feature(x):
    xf = x.astype(jnp.float32)
    return jnp.where(xf > 0, xf + 1.0, jnp.exp(jnp.minimum(xf, 0.0))).astype(jnp.bfloat16)


def add_states(earlier, later):
    return earlier + later


def on_device(queries, keys, values, keep, gain, out_weight):
    tok_rows = queries.shape[1]
    fq = feature(queries[0]).reshape(tok_rows, HEADS, HEAD)
    fk = feature(keys[0]).reshape(tok_rows, HEADS, HEAD)
    vals = values[0].reshape(tok_rows, HEADS, HEAD)
    state = jnp.einsum("thc,thd->hcd", fk, vals, preferred_element_type=jnp.float32)
    prefix = prefix_2(state, "seq", add_states, jnp.zeros_like(state))
    prefix = prefix.astype(jnp.bfloat16)
    inter = jnp.einsum("thc,hcd->thd", fq, prefix, preferred_element_type=jnp.float32)
    causal = jnp.arange(tok_rows)[:, None] >= jnp.arange(tok_rows)[None, :]
    scores = jnp.einsum("thc,shc->hts", fq, fk, preferred_element_type=jnp.float32)
    scores = jnp.where(causal[None], scores, 0.0).astype(jnp.bfloat16)
    intra = jnp.einsum("hts,shd->thd", scores, vals, preferred_element_type=jnp.float32)
    numer = inter + intra
    normed = (
        numer
        * lax.rsqrt(jnp.mean(numer * numer, axis=-1, keepdims=True) + 1e-06)
        * gain.reshape(HEADS, HEAD)
    )
    mask = keep[0].reshape(tok_rows, HEADS, HEAD).astype(jnp.float32)
    dropped = (normed * mask * (1.0 / 0.9)).astype(jnp.bfloat16).reshape(tok_rows, HEADS * HEAD)
    result = jnp.dot(
        dropped,
        lax.all_gather(out_weight, "dp", axis=1, tiled=True),
        preferred_element_type=jnp.float32,
    ).astype(jnp.bfloat16)
    return result[None]


def solution(mesh):
    return jax.shard_map(
        on_device,
        mesh=mesh,
        in_specs=(
            P("dp", "seq", None),
            P("dp", "seq", None),
            P("dp", "seq", None),
            P("dp", "seq", None),
            P(),
            P(None, "dp"),
        ),
        out_specs=P("dp", "seq", None),
        check_vma=False,
    )
```

profile of v0, /device:TPU:2, one launch (start us, length us, event | category | flops | bytes accessed | tf_op | source)
XLA Modules:
  0.0 313.0 jit_solution(7465845264773032418)
XLA Ops:
  6.5 1.5 fusion.16
  8.0 0.1 copy.27
  8.2 0.1 copy.28
  8.3 0.8 copy-done
  9.2 1.5 fusion.23
  10.8 0.7 all-gather.4.cloned.1.call-update
  11.5 1.5 fusion.15
  13.0 1.0 copy.26
  14.0 0.1 convert_bitcast_fusion
  14.1 0.2 copy.29
  14.4 3.3 %fusion.3 = f32[160,16,128]{2,0,1:T(8,128)} fusion(pred[160,160]{1,0:T(8,128)(4,1)S(1)} %iota_compare_fusion, bf16[160,16,128]{2,1,0:T(8,128)(2,1)} %bitcast.42, bf16[160,16,128]{2,1,0:T(8,128)(2,1)} %bitcast.41, bf16[160,16,128]{2,1,0:T(8,128)(2,1)S(1)} %bitcast.39), kind=kOutput, calls=%fused_computation.13 | convolution fusion | flops 210534400 | bytes 3302400 | tf_op jit(solution)/shard_map/hts,shd->thd/dot_general | solution.py:44
  17.7 188.8 %all-gather.6.cloned.1.call-done = f32[512,128,128]{2,1,0:T(8,128)} async-done(((f32[16,128,128]{2,1,0:T(8,128)}), f32[512,128,128]{2,1,0:T(8,128)}) %all-gather.6.cloned.1.call-update) | async-done | bytes 33554448 | tf_op jit(solution)/shard_map/all_gather | solution.py:12
  206.5 51.9 %while.14 = (s32[]{:T(128)}, f32[16,128,128]{2,1,0:T(8,128)S(1)}, s32[]{:T(128)}, f32[32,16,128,128]{3,2,1,0:T(8,128)}, s32[]{:T(128)}, /*index=5*/s32[]{:T(128)}) while((s32[]{:T(128)}, f32[16,128,128]{2,1,0:T(8,128)S(1)}, s32[]{:T(128)}, f32[32,16,128,128]{3,2,1,0:T(8,128)}, s32[]{:T(128)}, /*index=5*/s32[]{:T(128)}) %tuple.40), condition=%wide.region_1.2_spmd.clone, body=%wide.region_0.1_spmd.clone.sunk | while | flops 786436 | bytes 3145821 | solution.py:20
  206.5 1.7 add_select_fusion.2
  208.2 1.6 add_select_fusion.2
  209.8 1.6 add_select_fusion.2
  211.4 1.6 add_select_fusion.2
  213.0 1.6 add_select_fusion.2
  214.6 1.6 add_select_fusion.2
  216.2 1.6 add_select_fusion.2
  217.8 1.6 add_select_fusion.2
  219.5 1.6 add_select_fusion.2
  221.1 1.6 add_select_fusion.2
  222.7 1.6 add_select_fusion.2
  224.3 1.7 add_select_fusion.2
  226.0 1.6 add_select_fusion.2
  227.7 1.6 add_select_fusion.2
  229.3 1.6 add_select_fusion.2
  230.9 1.6 add_select_fusion.2
  232.5 1.6 add_select_fusion.2
  234.1 1.6 add_select_fusion.2
  235.8 1.6 add_select_fusion.2
  237.4 1.6 add_select_fusion.2
  239.0 1.6 add_select_fusion.2
  240.6 1.6 add_select_fusion.2
  242.2 1.6 add_select_fusion.2
  243.9 1.6 add_select_fusion.2
  245.5 1.6 add_select_fusion.2
  247.1 1.6 add_select_fusion.2
  248.7 1.6 add_select_fusion.2
  250.3 1.6 add_select_fusion.2
  251.9 1.6 add_select_fusion.2
  253.5 1.6 add_select_fusion.2
  255.2 1.6 add_select_fusion.2
  256.8 1.6 add_select_fusion.2
  258.4 3.1 multiply_reduce_fusion
  261.5 38.1 %all-gather.4.cloned.1.call-done = bf16[2048,2048]{1,0:T(8,128)(2,1)} async-done(((bf16[2048,128]{1,0:T(8,128)(2,1)}), bf16[2048,2048]{1,0:T(8,128)(2,1)}) %all-gather.4.cloned.1.call-update) | async-done | bytes 8388624 | tf_op jit(solution)/shard_map/all_gather | solution.py:55
  299.6 6.6 %fusion = bf16[1,160,2048]{2,1,0:T(8,128)(2,1)} fusion(bf16[2048,2048]{1,0:T(8,128)(2,1)} %all-gather.4.cloned.1.call-done, f32[160,16,128]{2,1,0:T(8,128)S(1)} %bitcast.37, f32[160,16,128]{2,0,1:T(8,128)} %get-tuple-element.109, f32[16,128]{1,0:T(8,128)S(1)} %bitcast.46, f32[160,16]{0,1:T(8,128)S(1)} %add_rsqrt_fusion), kind=kOutput, calls=%fused_computation.3 | convolution fusion | flops 1344143360 | bytes 11683840 | tf_op jit(solution)/shard_map/dot_general | solution.py:53
  (15 shorter events, 0.1 us)
Async XLA Ops:
  6.5 1.6 copy-start.3
  6.5 199.9 %all-gather.6.cloned.1.call-start = ((), (), s32[]{:S(2)}) async-start(), calls=%async_computation.1 | async-start | bytes 34603008 | tf_op jit(solution)/shard_map/all_gather | solution.py:12
  8.3 0.9 copy-start
  10.7 288.9 %all-gather.4.cloned.1.call-start = ((), (), s32[]{:S(2)}) async-start(), calls=%async_computation | async-start | bytes 8912896 | tf_op jit(solution)/shard_map/all_gather | solution.py:55
  11.5 2.5 copy-start.2
  206.5 51.9 %copy-start.1 = (bf16[20,8,16,128]{3,2,1,0:T(8,128)(2,1)S(1)}, bf16[20,8,16,128]{3,2,1,0:T(8,128)(2,1)}, u32[]{:S(2)}) copy-start(bf16[20,8,16,128]{3,2,1,0:T(8,128)(2,1)} %copy.26) | copy-start | bytes 1966084
  258.4 41.2 %copy-start.4 = (f32[2048]{0:T(1024)S(1)}, f32[2048]{0:T(1024)}, u32[]{:S(2)}) copy-start(f32[2048]{0:T(1024)} %param.12) | copy-start | bytes 24580
Sparse Core Ops, SparseCore 0:
  10.8 195.6 all-gather.5
  209.5 90.0 all-gather.3
where the time goes:
time: 314 us; the launch traced here: 313 us
  waiting for transfers between devices  228 us (73%)
  other arithmetic  54.3 us (17%)
  matrix products  14.4 us (5%)
  between operations  13.5 us (4%)
    all_gather x1, waiting for transfers between devices, prefix_2(): everything = lax.all_gather(x, axis)  189 us
    select_n x32, other arithmetic, turn(): return jnp.where(reached, new, before)  51.1 us
    all_gather x1, waiting for transfers between devices, on_device(): lax.all_gather(out_weight, 'dp', axis=1, tiled=True)  38.1 us
    dot_general x1, matrix products, on_device(): jnp.dot(dropped, lax.all_gather(out_weight, 'dp', axis=1, tiled=True), pr...  6.56 us
  transfers between devices with their start and end apart: 2, of which 2 were waited for; matrix products, arithmetic and copies ran while one was open for 19% of the time, Pallas kernels for 0%

commit v1 on v0

--- a/solution.py
+++ b/solution.py
@@ -50,11 +50,32 @@
     )
     mask = keep[0].reshape(tok_rows, HEADS, HEAD).astype(jnp.float32)
     dropped = (normed * mask * (1.0 / 0.9)).astype(jnp.bfloat16).reshape(tok_rows, HEADS * HEAD)
-    result = jnp.dot(
-        dropped,
-        lax.all_gather(out_weight, "dp", axis=1, tiled=True),
-        preferred_element_type=jnp.float32,
-    ).astype(jnp.bfloat16)
+
+    def _time_marks(u_in, chip_axis="dp"):
+        outer = lax.axis_size(chip_axis)
+        front = lax.axis_index(chip_axis)
+        clean, block_next, top = (outer, front, u_in.shape[1])
+        rack = tuple((w * clean if u == 1 else w for u, w in enumerate(u_in.shape)))
+        field_out = jnp.zeros(rack, u_in.dtype)
+        z_new = lax.dynamic_update_slice_in_dim(field_out, u_in, block_next * top, axis=1)
+        then = t1 = u_in
+        for k0 in [*range(1, clean // 2 + 1)]:
+            outcome_arr = tuple(((u, (u + 1) % clean) for u in range(clean)))
+            then = lax.ppermute(then, chip_axis, outcome_arr)
+            z_new = lax.dynamic_update_slice_in_dim(
+                z_new, then, (block_next - k0) % clean * top, axis=1
+            )
+            if 2 * k0 < clean:
+                long_array = tuple(((u, (u - 1) % clean) for u in range(clean)))
+                t1 = lax.ppermute(t1, chip_axis, perm=long_array)
+                z_new = lax.dynamic_update_slice_in_dim(
+                    z_new, t1, (block_next + k0) % clean * top, axis=1
+                )
+        return z_new
+
+    result = jnp.dot(dropped, _time_marks(out_weight), preferred_element_type=jnp.float32).astype(
+        jnp.bfloat16
+    )
     return result[None]
 
 

time: 314 us -> 277 us (0.88)
  the two profiles are of different devices: /device:TPU:2 before, /device:TPU:1 now
where the time goes in v1:
time: 277 us; the launch traced here: 275 us
  waiting for transfers between devices  100 us (36%)
  starting transfers between devices  65.5 us (24%)
  other arithmetic  55 us (20%)
  local copies, waits for them, and re-layouts  27.8 us (10%)
  between operations  13.7 us (5%)
  matrix products  11.7 us (4%)
    all_gather x1, waiting for transfers between devices, prefix_2(): everything = lax.all_gather(x, axis)  75.6 us
    select_n x32, other arithmetic, turn(): return jnp.where(reached, new, before)  50.9 us
    ppermute x7, starting transfers between devices, _time_marks(): t1 = lax.ppermute(t1, chip_axis, perm=long_array)  45.1 us
    ppermute x8, waiting for transfers between devices, _time_marks(): then = lax.ppermute(then, chip_axis, outcome_arr)  20.7 us
    ppermute x8, starting transfers between devices, _time_marks(): then = lax.ppermute(then, chip_axis, outcome_arr)  20.4 us
    dynamic_update_slice x8, local copies, waits for them, and re-layouts, _time_marks(): lax.dynamic_update_slice_in_dim(z_new, then, (block_next - k0) % clean *...  11.4 us
    dynamic_update_slice x7, local copies, waits for them, and re-layouts, _time_marks(): lax.dynamic_update_slice_in_dim(z_new, t1, (block_next + k0) % clean * to...  8.26 us
    dot_general x1, matrix products, on_device(): jnp.dot(dropped, _time_marks(out_weight), preferred_element_type=jnp.floa...  6.16 us
  transfers between devices with their start and end apart: 16, of which 9 were waited for; matrix products, arithmetic and copies ran while one was open for 11% of the time, Pallas kernels for 0%

profile of v1, /device:TPU:1, one launch (start us, length us, event | category | flops | bytes accessed | tf_op | source)
XLA Modules:
  0.0 274.8 jit_solution(17946082432777871720)
XLA Ops:
  11.0 4.0 %collective-permute-start = (bf16[2048,128]{1,0:T(8,128)(2,1)}, bf16[2048,128]{1,0:T(8,128)(2,1)S(1)}, u32[]{:S(2)}, u32[]{:S(2)}) collective-permute-start(bf16[2048,128]{1,0:T(8,128)(2,1)} %param.13), channel_id=1, source_target_pairs={{0,1},{1,2},{2,3},{3,4},{4,5},{5,6},{6,7},{7,8},{8,9},{9,10},{10,1... | collective-permute-start | bytes 1572872 | tf_op jit(solution)/shard_map/ppermute | solution.py:64
  15.0 5.6 %collective-permute-start.1 = (bf16[2048,128]{1,0:T(8,128)(2,1)}, bf16[2048,128]{1,0:T(8,128)(2,1)}, u32[]{:S(2)}, u32[]{:S(2)}) collective-permute-start(bf16[2048,128]{1,0:T(8,128)(2,1)} %param.13), channel_id=1, source_target_pairs={{0,15},{1,0},{2,1},{3,2},{4,3},{5,4},{6,5},{7,6},{8,7},{9,8},{10,9... | collective-permute-start | bytes 1572872 | tf_op jit(solution)/shard_map/ppermute | solution.py:70
  20.6 4.8 %collective-permute-done = bf16[2048,128]{1,0:T(8,128)(2,1)S(1)} collective-permute-done((bf16[2048,128]{1,0:T(8,128)(2,1)}, bf16[2048,128]{1,0:T(8,128)(2,1)S(1)}, u32[]{:S(2)}, u32[]{:S(2)}) %collective-permute-start) | collective-permute-done | bytes 524320 | tf_op jit(solution)/shard_map/ppermute | solution.py:64
  25.4 3.7 %collective-permute-start.2 = (bf16[2048,128]{1,0:T(8,128)(2,1)S(1)}, bf16[2048,128]{1,0:T(8,128)(2,1)}, u32[]{:S(2)}, u32[]{:S(2)}) collective-permute-start(bf16[2048,128]{1,0:T(8,128)(2,1)S(1)} %collective-permute-done), channel_id=1, source_target_pairs={{0,1},{1,2},{2,3},{3,4},{4,5},{5,6},{6,7},{7,8},{8,9},{9,10},{10,1... | collective-permute-start | bytes 1572872 | tf_op jit(solution)/shard_map/ppermute | solution.py:64
  29.1 6.3 %collective-permute-start.3 = (bf16[2048,128]{1,0:T(8,128)(2,1)}, bf16[2048,128]{1,0:T(8,128)(2,1)}, u32[]{:S(2)}, u32[]{:S(2)}) collective-permute-start(bf16[2048,128]{1,0:T(8,128)(2,1)} %collective-permute-done.1), channel_id=1, source_target_pairs={{0,15},{1,0},{2,1},{3,2},{4,3},{5,4},{6,5},{7,6},{8,7},{9,8},{10,9... | collective-permute-start | bytes 1572872 | tf_op jit(solution)/shard_map/ppermute | solution.py:70
  37.1 3.1 %collective-permute-done.2 = bf16[2048,128]{1,0:T(8,128)(2,1)} collective-permute-done((bf16[2048,128]{1,0:T(8,128)(2,1)S(1)}, bf16[2048,128]{1,0:T(8,128)(2,1)}, u32[]{:S(2)}, u32[]{:S(2)}) %collective-permute-start.2) | collective-permute-done | bytes 524320 | tf_op jit(solution)/shard_map/ppermute | solution.py:64
  40.2 2.8 %collective-permute-start.4 = (bf16[2048,128]{1,0:T(8,128)(2,1)}, bf16[2048,128]{1,0:T(8,128)(2,1)}, u32[]{:S(2)}, u32[]{:S(2)}) collective-permute-start(bf16[2048,128]{1,0:T(8,128)(2,1)} %collective-permute-done.2), channel_id=1, source_target_pairs={{0,1},{1,2},{2,3},{3,4},{4,5},{5,6},{6,7},{7,8},{8,9},{9,10},{10,1... | collective-permute-start | bytes 1572872 | tf_op jit(solution)/shard_map/ppermute | solution.py:64
  43.0 2.0 fusion.3
  45.0 6.5 %collective-permute-start.5 = (bf16[2048,128]{1,0:T(8,128)(2,1)}, bf16[2048,128]{1,0:T(8,128)(2,1)S(1)}, u32[]{:S(2)}, u32[]{:S(2)}) collective-permute-start(bf16[2048,128]{1,0:T(8,128)(2,1)} %collective-permute-done.3), channel_id=1, source_target_pairs={{0,15},{1,0},{2,1},{3,2},{4,3},{5,4},{6,5},{7,6},{8,7},{9,8},{10,9... | collective-permute-start | bytes 1572872 | tf_op jit(solution)/shard_map/ppermute | solution.py:70
  52.6 1.7 collective-permute-done.4
  54.3 2.2 collective-permute-start.6
  56.5 4.3 %broadcast_in_dim.28 = bf16[2048,2048]{1,0:T(8,128)(2,1)} broadcast(bf16[]{:T(256)} %constant.130.clone.1), dimensions={} | broadcast | bytes 8388610 | tf_op jit(solution)/shard_map/broadcast_in_dim | solution.py:59
  63.3 2.0 constant_dynamic-update-slice_fusion.14
  65.3 6.4 %collective-permute-start.7 = (bf16[2048,128]{1,0:T(8,128)(2,1)S(1)}, bf16[2048,128]{1,0:T(8,128)(2,1)S(1)}, u32[]{:S(2)}, u32[]{:S(2)}) collective-permute-start(bf16[2048,128]{1,0:T(8,128)(2,1)S(1)} %collective-permute-done.5), channel_id=1, source_target_pairs={{0,15},{1,0},{2,1},{3,2},{4,3},{5,4},{6,5},{7,6},{8,7},{9,8},{10,9... | collective-permute-start | bytes 1572872 | tf_op jit(solution)/shard_map/ppermute | solution.py:70
  71.7 1.9 constant_dynamic-update-slice_fusion.13
  73.7 1.9 collective-permute-start.8
  75.6 1.9 constant_dynamic-update-slice_fusion.12
  77.5 1.9 constant_dynamic-update-slice_fusion.11
  79.4 6.6 %collective-permute-start.9 = (bf16[2048,128]{1,0:T(8,128)(2,1)S(1)}, bf16[2048,128]{1,0:T(8,128)(2,1)S(1)}, u32[]{:S(2)}, u32[]{:S(2)}) collective-permute-start(bf16[2048,128]{1,0:T(8,128)(2,1)S(1)} %collective-permute-done.7), channel_id=1, source_target_pairs={{0,15},{1,0},{2,1},{3,2},{4,3},{5,4},{6,5},{7,6},{8,7},{9,8},{10,9... | collective-permute-start | bytes 1572872 | tf_op jit(solution)/shard_map/ppermute | solution.py:70
  86.1 1.9 constant_dynamic-update-slice_fusion.10
  88.0 1.9 collective-permute-start.10
  90.8 2.0 constant_dynamic-update-slice_fusion.8
  92.8 6.6 %collective-permute-start.11 = (bf16[2048,128]{1,0:T(8,128)(2,1)S(1)}, bf16[2048,128]{1,0:T(8,128)(2,1)S(1)}, u32[]{:S(2)}, u32[]{:S(2)}) collective-permute-start(bf16[2048,128]{1,0:T(8,128)(2,1)S(1)} %collective-permute-done.9), channel_id=1, source_target_pairs={{0,15},{1,0},{2,1},{3,2},{4,3},{5,4},{6,5},{7,6},{8,7},{9,8},{10,9... | collective-permute-start | bytes 1572872 | tf_op jit(solution)/shard_map/ppermute | solution.py:70
  101.2 1.9 collective-permute-start.12
  106.4 7.1 %collective-permute-start.13 = (bf16[2048,128]{1,0:T(8,128)(2,1)S(1)}, bf16[2048,128]{1,0:T(8,128)(2,1)S(1)}, u32[]{:S(2)}, u32[]{:S(2)}) collective-permute-start(bf16[2048,128]{1,0:T(8,128)(2,1)S(1)} %collective-permute-done.11), channel_id=1, source_target_pairs={{0,15},{1,0},{2,1},{3,2},{4,3},{5,4},{6,5},{7,6},{8,7},{9,8},{10,9... | collective-permute-start | bytes 1572872 | tf_op jit(solution)/shard_map/ppermute | solution.py:70
  115.7 1.9 collective-permute-start.14
  119.4 2.4 collective-permute-done.13
  122.6 8.8 %collective-permute-done.14 = bf16[2048,128]{1,0:T(8,128)(2,1)S(1)} collective-permute-done((bf16[2048,128]{1,0:T(8,128)(2,1)S(1)}, bf16[2048,128]{1,0:T(8,128)(2,1)S(1)}, u32[]{:S(2)}, u32[]{:S(2)}) %collective-permute-start.14) | collective-permute-done | bytes 524320 | tf_op jit(solution)/shard_map/ppermute | solution.py:64
  132.4 75.6 %all-gather.3.cloned.1.call-done = f32[512,128,128]{2,1,0:T(8,128)} async-done(((f32[16,128,128]{2,1,0:T(8,128)}), f32[512,128,128]{2,1,0:T(8,128)}) %all-gather.3.cloned.1.call-update) | async-done | bytes 33554448 | tf_op jit(solution)/shard_map/all_gather | solution.py:12
  208.0 51.6 %while.14 = (s32[]{:T(128)}, f32[16,128,128]{2,1,0:T(8,128)S(1)}, s32[]{:T(128)}, f32[32,16,128,128]{3,2,1,0:T(8,128)}, s32[]{:T(128)}, /*index=5*/s32[]{:T(128)}) while((s32[]{:T(128)}, f32[16,128,128]{2,1,0:T(8,128)S(1)}, s32[]{:T(128)}, f32[32,16,128,128]{3,2,1,0:T(8,128)}, s32[]{:T(128)}, /*index=5*/s32[]{:T(128)}) %tuple.38), condition=%wide.region_1.2_spmd.clone, body=%wide.region_0.1_spmd.clone.sunk | while | flops 786436 | bytes 3145821 | solution.py:20
  208.0 1.6 add_select_fusion.2
  209.6 1.6 add_select_fusion.2
  211.2 1.6 add_select_fusion.2
  212.8 1.6 add_select_fusion.2
  214.5 1.6 add_select_fusion.2
  217.7 1.6 add_select_fusion.2
  219.3 1.6 add_select_fusion.2
  220.9 1.6 add_select_fusion.2
  225.8 1.6 add_select_fusion.2
  227.4 1.6 add_select_fusion.2
  229.0 1.6 add_select_fusion.2
  233.8 1.6 add_select_fusion.2
  235.4 1.6 add_select_fusion.2
  237.0 1.6 add_select_fusion.2
  240.3 1.6 add_select_fusion.2
  241.9 1.6 add_select_fusion.2
  259.6 2.1 multiply_reduce_fusion
  261.8 6.2 %fusion = bf16[1,160,2048]{2,1,0:T(8,128)(2,1)} fusion(bf16[2048,2048]{1,0:T(8,128)(2,1)} %constant_dynamic-update-slice_fusion, f32[160,16,128]{2,1,0:T(8,128)S(1)} %bitcast.37, f32[160,16,128]{2,0,1:T(8,128)S(1)} %get-tuple-element.109, f32[16,128]{1,0:T(8,128)S(1)} %bitcast.46, f32[160,16]{0,1:T(8,128)S(1)} %add_rsqrt_fusion), kind=kOutput, calls=%fused_computation.3 | convolution fusion | flops 1344143360 | bytes 11683840 | tf_op jit(solution)/shard_map/dot_general | solution.py:76
  (57 shorter events, 46.7 us)
Async XLA Ops:
  6.5 44.9 %copy-start = (s32[1,160,2048]{2,1,0:T(8,128)S(1)}, s32[1,160,2048]{2,1,0:T(8,128)}, u32[]{:S(2)}) copy-start(s32[1,160,2048]{2,1,0:T(8,128)} %param.11) | copy-start | bytes 3932164
  6.5 201.5 %all-gather.3.cloned.1.call-start = ((), (), s32[]{:S(2)}) async-start(), calls=%async_computation | async-start | bytes 34603008 | tf_op jit(solution)/shard_map/all_gather | solution.py:12
  11.0 14.4 %collective-permute-start = (bf16[2048,128]{1,0:T(8,128)(2,1)}, bf16[2048,128]{1,0:T(8,128)(2,1)S(1)}, u32[]{:S(2)}, u32[]{:S(2)}) collective-permute-start(bf16[2048,128]{1,0:T(8,128)(2,1)} %param.13), channel_id=1, source_target_pairs={{0,1},{1,2},{2,3},{3,4},{4,5},{5,6},{6,7},{7,8},{8,9},{9,10},{10,1... | collective-permute-start | bytes 1572872 | tf_op jit(solution)/shard_map/ppermute | solution.py:64
  15.0 14.1 %collective-permute-start.1 = (bf16[2048,128]{1,0:T(8,128)(2,1)}, bf16[2048,128]{1,0:T(8,128)(2,1)}, u32[]{:S(2)}, u32[]{:S(2)}) collective-permute-start(bf16[2048,128]{1,0:T(8,128)(2,1)} %param.13), channel_id=1, source_target_pairs={{0,15},{1,0},{2,1},{3,2},{4,3},{5,4},{6,5},{7,6},{8,7},{9,8},{10,9... | collective-permute-start | bytes 1572872 | tf_op jit(solution)/shard_map/ppermute | solution.py:70
  25.4 11.7 %copy-start.2 = (bf16[2048,128]{1,0:T(8,128)(2,1)}, bf16[2048,128]{1,0:T(8,128)(2,1)S(1)}, u32[]{:S(2)}) copy-start(bf16[2048,128]{1,0:T(8,128)(2,1)S(1)} %collective-permute-done) | copy-start | bytes 1572868
  25.4 14.8 %collective-permute-start.2 = (bf16[2048,128]{1,0:T(8,128)(2,1)S(1)}, bf16[2048,128]{1,0:T(8,128)(2,1)}, u32[]{:S(2)}, u32[]{:S(2)}) collective-permute-start(bf16[2048,128]{1,0:T(8,128)(2,1)S(1)} %collective-permute-done), channel_id=1, source_target_pairs={{0,1},{1,2},{2,3},{3,4},{4,5},{5,6},{6,7},{7,8},{8,9},{9,10},{10,1... | collective-permute-start | bytes 1572872 | tf_op jit(solution)/shard_map/ppermute | solution.py:64
  29.1 15.9 %collective-permute-start.3 = (bf16[2048,128]{1,0:T(8,128)(2,1)}, bf16[2048,128]{1,0:T(8,128)(2,1)}, u32[]{:S(2)}, u32[]{:S(2)}) collective-permute-start(bf16[2048,128]{1,0:T(8,128)(2,1)} %collective-permute-done.1), channel_id=1, source_target_pairs={{0,15},{1,0},{2,1},{3,2},{4,3},{5,4},{6,5},{7,6},{8,7},{9,8},{10,9... | collective-permute-start | bytes 1572872 | tf_op jit(solution)/shard_map/ppermute | solution.py:70
  40.2 14.1 %collective-permute-start.4 = (bf16[2048,128]{1,0:T(8,128)(2,1)}, bf16[2048,128]{1,0:T(8,128)(2,1)}, u32[]{:S(2)}, u32[]{:S(2)}) collective-permute-start(bf16[2048,128]{1,0:T(8,128)(2,1)} %collective-permute-done.2), channel_id=1, source_target_pairs={{0,1},{1,2},{2,3},{3,4},{4,5},{5,6},{6,7},{7,8},{8,9},{9,10},{10,1... | collective-permute-start | bytes 1572872 | tf_op jit(solution)/shard_map/ppermute | solution.py:64
  45.0 15.9 %copy-start.1 = (bf16[2048,128]{1,0:T(8,128)(2,1)S(1)}, bf16[2048,128]{1,0:T(8,128)(2,1)}, u32[]{:S(2)}) copy-start(bf16[2048,128]{1,0:T(8,128)(2,1)} %param.13) | copy-start | bytes 1572868
  45.0 20.3 %collective-permute-start.5 = (bf16[2048,128]{1,0:T(8,128)(2,1)}, bf16[2048,128]{1,0:T(8,128)(2,1)S(1)}, u32[]{:S(2)}, u32[]{:S(2)}) collective-permute-start(bf16[2048,128]{1,0:T(8,128)(2,1)} %collective-permute-done.3), channel_id=1, source_target_pairs={{0,15},{1,0},{2,1},{3,2},{4,3},{5,4},{6,5},{7,6},{8,7},{9,8},{10,9... | collective-permute-start | bytes 1572872 | tf_op jit(solution)/shard_map/ppermute | solution.py:70
  54.3 19.3 %collective-permute-start.6 = (bf16[2048,128]{1,0:T(8,128)(2,1)}, bf16[2048,128]{1,0:T(8,128)(2,1)}, u32[]{:S(2)}, u32[]{:S(2)}) collective-permute-start(bf16[2048,128]{1,0:T(8,128)(2,1)} %collective-permute-done.4), channel_id=1, source_target_pairs={{0,1},{1,2},{2,3},{3,4},{4,5},{5,6},{6,7},{7,8},{8,9},{9,10},{10,1... | collective-permute-start | bytes 1572872 | tf_op jit(solution)/shard_map/ppermute | solution.py:64
  65.3 14.1 %collective-permute-start.7 = (bf16[2048,128]{1,0:T(8,128)(2,1)S(1)}, bf16[2048,128]{1,0:T(8,128)(2,1)S(1)}, u32[]{:S(2)}, u32[]{:S(2)}) collective-permute-start(bf16[2048,128]{1,0:T(8,128)(2,1)S(1)} %collective-permute-done.5), channel_id=1, source_target_pairs={{0,15},{1,0},{2,1},{3,2},{4,3},{5,4},{6,5},{7,6},{8,7},{9,8},{10,9... | collective-permute-start | bytes 1572872 | tf_op jit(solution)/shard_map/ppermute | solution.py:70
  73.7 14.3 %collective-permute-start.8 = (bf16[2048,128]{1,0:T(8,128)(2,1)}, bf16[2048,128]{1,0:T(8,128)(2,1)S(1)}, u32[]{:S(2)}, u32[]{:S(2)}) collective-permute-start(bf16[2048,128]{1,0:T(8,128)(2,1)} %collective-permute-done.6), channel_id=1, source_target_pairs={{0,1},{1,2},{2,3},{3,4},{4,5},{5,6},{6,7},{7,8},{8,9},{9,10},{10,1... | collective-permute-start | bytes 1572872 | tf_op jit(solution)/shard_map/ppermute | solution.py:64
  79.4 13.4 %collective-permute-start.9 = (bf16[2048,128]{1,0:T(8,128)(2,1)S(1)}, bf16[2048,128]{1,0:T(8,128)(2,1)S(1)}, u32[]{:S(2)}, u32[]{:S(2)}) collective-permute-start(bf16[2048,128]{1,0:T(8,128)(2,1)S(1)} %collective-permute-done.7), channel_id=1, source_target_pairs={{0,15},{1,0},{2,1},{3,2},{4,3},{5,4},{6,5},{7,6},{8,7},{9,8},{10,9... | collective-permute-start | bytes 1572872 | tf_op jit(solution)/shard_map/ppermute | solution.py:70
  88.0 13.2 %collective-permute-start.10 = (bf16[2048,128]{1,0:T(8,128)(2,1)S(1)}, bf16[2048,128]{1,0:T(8,128)(2,1)S(1)}, u32[]{:S(2)}, u32[]{:S(2)}) collective-permute-start(bf16[2048,128]{1,0:T(8,128)(2,1)S(1)} %collective-permute-done.8), channel_id=1, source_target_pairs={{0,1},{1,2},{2,3},{3,4},{4,5},{5,6},{6,7},{7,8},{8,9},{9,10},{10,1... | collective-permute-start | bytes 1572872 | tf_op jit(solution)/shard_map/ppermute | solution.py:64
  92.8 13.6 %collective-permute-start.11 = (bf16[2048,128]{1,0:T(8,128)(2,1)S(1)}, bf16[2048,128]{1,0:T(8,128)(2,1)S(1)}, u32[]{:S(2)}, u32[]{:S(2)}) collective-permute-start(bf16[2048,128]{1,0:T(8,128)(2,1)S(1)} %collective-permute-done.9), channel_id=1, source_target_pairs={{0,15},{1,0},{2,1},{3,2},{4,3},{5,4},{6,5},{7,6},{8,7},{9,8},{10,9... | collective-permute-start | bytes 1572872 | tf_op jit(solution)/shard_map/ppermute | solution.py:70
  101.2 14.5 %collective-permute-start.12 = (bf16[2048,128]{1,0:T(8,128)(2,1)S(1)}, bf16[2048,128]{1,0:T(8,128)(2,1)S(1)}, u32[]{:S(2)}, u32[]{:S(2)}) collective-permute-start(bf16[2048,128]{1,0:T(8,128)(2,1)S(1)} %collective-permute-done.10), channel_id=1, source_target_pairs={{0,1},{1,2},{2,3},{3,4},{4,5},{5,6},{6,7},{7,8},{8,9},{9,10},{10,1... | collective-permute-start | bytes 1572872 | tf_op jit(solution)/shard_map/ppermute | solution.py:64
  106.4 15.3 %collective-permute-start.13 = (bf16[2048,128]{1,0:T(8,128)(2,1)S(1)}, bf16[2048,128]{1,0:T(8,128)(2,1)S(1)}, u32[]{:S(2)}, u32[]{:S(2)}) collective-permute-start(bf16[2048,128]{1,0:T(8,128)(2,1)S(1)} %collective-permute-done.11), channel_id=1, source_target_pairs={{0,15},{1,0},{2,1},{3,2},{4,3},{5,4},{6,5},{7,6},{8,7},{9,8},{10,9... | collective-permute-start | bytes 1572872 | tf_op jit(solution)/shard_map/ppermute | solution.py:70
  115.7 15.7 %collective-permute-start.14 = (bf16[2048,128]{1,0:T(8,128)(2,1)S(1)}, bf16[2048,128]{1,0:T(8,128)(2,1)S(1)}, u32[]{:S(2)}, u32[]{:S(2)}) collective-permute-start(bf16[2048,128]{1,0:T(8,128)(2,1)S(1)} %collective-permute-done.12), channel_id=1, source_target_pairs={{0,1},{1,2},{2,3},{3,4},{4,5},{5,6},{6,7},{7,8},{8,9},{9,10},{10,1... | collective-permute-start | bytes 1572872 | tf_op jit(solution)/shard_map/ppermute | solution.py:64
  208.0 53.8 %copy-start.3 = (f32[2048]{0:T(1024)S(1)}, f32[2048]{0:T(1024)}, u32[]{:S(2)}) copy-start(f32[2048]{0:T(1024)} %param.12) | copy-start | bytes 24580
Sparse Core Ops, SparseCore 0:
  11.1 196.8 all-gather.2
